TPU v7x, 32 devices: a whole 2x2x4 slice. The times are simulated.
32 devices in a mesh: groups: 2 (over y), row: 4 (over x, core), col: 4 (over z).
Axes of the slice: x: 2, y: 2, z: 4, core: 2. Of those that a mesh axis runs over, the one named last changes fastest.
Arguments:
- inputs: bfloat16 [1536, 4096], P(('groups', 'col'), 'row'), parts along dimension 0, may hold values from -6 to 6
- cotangent: bfloat16 [1536, 4096], P(('groups', 'col'), 'row'), parts along dimension 0, may hold values from -6 to 6
- preactivation: bfloat16 [1536, 8192], P(('groups', 'row'), 'col'), parts along dimension 0, may hold values from -8 to 8
- up_weight: bfloat16 [4096, 8192], P('row', 'col'), may hold values from -0.09375 to 0.09375
- down_weight: bfloat16 [8192, 4096], P('col', 'row'), may hold values from -0.0625 to 0.0625
Outputs:
- grad_input: bfloat16 [1536, 4096], P(('groups', 'col'), 'row'), parts along dimension 0
- grad_up: float32 [8192, 8192], P(('groups', 'row'), 'col'), parts along dimension 0
- grad_down: float32 [16384, 4096], P(('groups', 'col'), 'row'), parts along dimension 0
There are 2 independent parts, one for each index of `groups`. A program takes and returns all parts, laid end to end along the dimension named above; an argument that names none is the same for every part. Nothing has to cross between parts.
All inputs are finite; a program needn't handle non-finite values.
Results may differ from a plain program's by a relative error of at most 0.0049.
Values may be sent and summed in bfloat16 or wider, within the bound.
A program may use at most 128 MiB of HBM per device.

v0:
```python
import math
import jax
import jax.numpy as jnp
from jax import lax
from jax.sharding import PartitionSpec as P


def gelu_pair(values):
    v = values.astype(jnp.float32)
    tanh_arg = 0.7978845608 * (v + 0.044715 * v * v * v)
    tanh_val = jnp.tanh(tanh_arg)
    gelu_value = 0.5 * v * (1.0 + tanh_val)
    gelu_slope = 0.5 * (1.0 + tanh_val) + 0.5 * v * (1.0 - tanh_val * tanh_val) * 0.7978845608 * (
        1.0 + 3.0 * 0.044715 * v * v
    )
    return (gelu_value, gelu_slope)


def per_device(inputs, cotangent, preactivation, up_weight, down_weight):
    inputs_all, cotangent_all = (
        lax.all_gather(inputs, "col", axis=0, tiled=True),
        lax.all_gather(cotangent, "col", axis=0, tiled=True),
    )
    total_tokens = inputs_all.shape[0]
    token_scale = 1.0 / math.sqrt(total_tokens)
    last_dims = (((1,), (1,)), ((), ()))
    first_dims = (((0,), (0,)), ((), ()))
    piece = cotangent_all
    hidden_grad = lax.psum_scatter(
        lax.dot_general(piece, down_weight, last_dims, preferred_element_type=jnp.float32),
        "row",
        scatter_dimension=0,
        tiled=True,
    )
    gelu_value, gelu_slope = gelu_pair(preactivation)
    activation = gelu_value.astype(jnp.bfloat16)
    pre_grad = (hidden_grad * gelu_slope).astype(jnp.bfloat16)
    activation_all, pre_grad_all = (
        lax.all_gather(activation, "row", axis=0, tiled=True),
        lax.all_gather(pre_grad, "row", axis=0, tiled=True),
    )
    piece = pre_grad_all
    grad_input = lax.psum_scatter(
        lax.dot_general(piece, up_weight, last_dims, preferred_element_type=jnp.float32),
        "col",
        scatter_dimension=0,
        tiled=True,
    ).astype(jnp.bfloat16)
    grad_up = (
        lax.dot_general(inputs_all, pre_grad_all, first_dims, preferred_element_type=jnp.float32)
        * token_scale
    )
    grad_down = (
        lax.dot_general(
            activation_all, cotangent_all, first_dims, preferred_element_type=jnp.float32
        )
        * token_scale
    )
    return (grad_input, grad_up, grad_down)


def solution(mesh):
    placed = (
        P(("groups", "col"), "row"),
        P(("groups", "col"), "row"),
        P(("groups", "row"), "col"),
        P("row", "col"),
        P("col", "row"),
    )
    return jax.shard_map(
        per_device,
        mesh=mesh,
        in_specs=placed,
        out_specs=(
            P(("groups", "col"), "row"),
            P(("groups", "row"), "col"),
            P(("groups", "col"), "row"),
        ),
        check_vma=False,
    )
```

profile of v0, /device:TPU:0, one launch (start us, length us, event | category | flops | bytes accessed | tf_op | source)
XLA Modules:
  0.0 287.1 jit_solution(9059382792913873849)
XLA Ops:
  7.2 0.0 all-gather.5.cloned.1.call-start
  7.2 0.7 all-gather.5.cloned.1.call-update
  7.9 0.0 reduce-scatter.3.cloned.1.call-start
  7.9 41.4 %all-gather.5.cloned.1.call-done = bf16[768,1024]{1,0:T(8,128)(2,1)} async-done(((bf16[192,1024]{1,0:T(8,128)(2,1)}), bf16[768,1024]{1,0:T(8,128)(2,1)}) %all-gather.5.cloned.1.call-update) | async-done | bytes 1572880 | tf_op jit(solution)/shard_map/all_gather | solution.py:22
  49.3 8.8 %fusion.11 = f32[768,2048]{1,0:T(8,128)} fusion(bf16[768,1024]{1,0:T(8,128)(2,1)} %all-gather.5.cloned.1.call-done, bf16[2048,1024]{1,0:T(8,128)(2,1)} %param.9), kind=kOutput, calls=%fused_computation.20 | convolution fusion | flops 3221225472 | bytes 12058624 | tf_op jit(solution)/shard_map/dot_general | solution.py:30
  58.1 0.0 copy-start
  58.1 0.0 reduce-scatter.3.cloned.1.call-update
  58.2 0.0 all-gather.7.cloned.1.call-start
  58.2 57.8 %reduce-scatter.3.cloned.1.call-done = f32[192,2048]{1,0:T(8,128)} async-done(((f32[768,2048]{1,0:T(8,128)}), f32[192,2048]{1,0:T(8,128)}) %reduce-scatter.3.cloned.1.call-update) | async-done | bytes 1572880 | tf_op jit(solution)/shard_map/reduce_scatter | solution.py:29
  116.0 0.0 copy-done
  116.0 3.7 %fusion.7 = (bf16[192,2048]{1,0:T(8,128)(2,1)}, bf16[192,2048]{1,0:T(8,128)(2,1)}) fusion(bf16[192,2048]{1,0:T(8,128)(2,1)S(1)} %copy-done, f32[192,2048]{1,0:T(8,128)} %reduce-scatter.3.cloned.1.call-done), kind=kLoop, calls=%fused_computation.16 | loop fusion | flops 8650752 | bytes 3932160 | tf_op jit(solution)/shard_map/convert_element_type | solution.py:36
  119.7 0.0 all-gather.7.cloned.1.call-update
  119.7 0.0 all-gather.9.cloned.1.call-start
  119.8 0.5 all-gather.9.cloned.1.call-update
  120.3 0.0 all-gather.11.cloned.1.call-start
  120.4 0.5 all-gather.11.cloned.1.call-update
  120.9 0.0 reduce-scatter.5.cloned.1.call-start
  121.0 27.4 %all-gather.7.cloned.1.call-done = bf16[768,2048]{1,0:T(8,128)(2,1)} async-done(((bf16[192,2048]{1,0:T(8,128)(2,1)}), bf16[768,2048]{1,0:T(8,128)(2,1)}) %all-gather.7.cloned.1.call-update) | async-done | bytes 3145744 | tf_op jit(solution)/shard_map/all_gather | solution.py:40
  148.4 8.3 %fusion.12 = f32[768,1024]{1,0:T(8,128)} fusion(bf16[768,2048]{1,0:T(8,128)(2,1)} %all-gather.7.cloned.1.call-done, bf16[1024,2048]{1,0:T(8,128)(2,1)} %param.8), kind=kOutput, calls=%fused_computation.21 | convolution fusion | flops 3221225472 | bytes 10485760 | tf_op jit(solution)/shard_map/dot_general | solution.py:44
  156.7 0.0 copy-start.1
  156.7 0.0 reduce-scatter.5.cloned.1.call-update
  156.7 30.2 %all-gather.9.cloned.1.call-done = bf16[768,1024]{1,0:T(8,128)(2,1)} async-done(((bf16[192,1024]{1,0:T(8,128)(2,1)}), bf16[768,1024]{1,0:T(8,128)(2,1)}) %all-gather.9.cloned.1.call-update) | async-done | bytes 1572880 | tf_op jit(solution)/shard_map/all_gather | solution.py:21
  186.9 0.0 copy-done.1
  186.9 7.1 %multiply_bitcast_fusion = f32[1024,2048]{0,1:T(8,128)} fusion(bf16[768,2048]{1,0:T(8,128)(2,1)S(1)} %copy-done.1, bf16[768,1024]{1,0:T(8,128)(2,1)} %all-gather.9.cloned.1.call-done), kind=kOutput, calls=%fused_computation | convolution fusion | flops 3223322624 | bytes 13107200 | tf_op jit(solution)/shard_map/dot_general | solution.py:50
  194.0 0.0 copy-start.2
  194.0 9.4 %copy.8 = f32[1024,2048]{1,0:T(8,128)} copy(f32[1024,2048]{0,1:T(8,128)} %multiply_bitcast_fusion) | data formatting | bytes 16777216
  203.4 12.3 %all-gather.11.cloned.1.call-done = bf16[768,2048]{1,0:T(8,128)(2,1)} async-done(((bf16[192,2048]{1,0:T(8,128)(2,1)}), bf16[768,2048]{1,0:T(8,128)(2,1)}) %all-gather.11.cloned.1.call-update) | async-done | bytes 3145744 | tf_op jit(solution)/shard_map/all_gather | solution.py:39
  215.7 0.0 copy-done.2
  215.7 7.6 %convolution_multiply_fusion = f32[2048,1024]{1,0:T(8,128)} fusion(bf16[768,2048]{1,0:T(8,128)(2,1)} %all-gather.11.cloned.1.call-done, bf16[768,1024]{1,0:T(8,128)(2,1)S(1)} %copy-done.2), kind=kOutput, calls=%fused_computation.1 | convolution fusion | flops 3223322624 | bytes 13107200 | tf_op jit(solution)/shard_map/dot_general | solution.py:54
  223.3 55.0 %reduce-scatter.5.cloned.1.call-done = f32[192,1024]{1,0:T(8,128)} async-done(((f32[768,1024]{1,0:T(8,128)}), f32[192,1024]{1,0:T(8,128)}) %reduce-scatter.5.cloned.1.call-update) | async-done | bytes 786448 | tf_op jit(solution)/shard_map/reduce_scatter | solution.py:43
  278.3 1.9 convert_element_type.14
Async XLA Ops:
  7.2 42.2 %all-gather.5.cloned.1.call-start = ((), (), s32[]{:S(2)}) async-start(), calls=%async_computation.2 | async-start | bytes 1966080 | tf_op jit(solution)/shard_map/all_gather | solution.py:22
  7.9 108.1 %reduce-scatter.3.cloned.1.call-start = ((), (), s32[]{:S(2)}) async-start(), calls=%async_computation.3 | async-start | bytes 7864320 | tf_op jit(solution)/shard_map/reduce_scatter | solution.py:29
  58.1 57.9 %copy-start = (bf16[192,2048]{1,0:T(8,128)(2,1)S(1)}, bf16[192,2048]{1,0:T(8,128)(2,1)}, u32[]{:S(2)}) copy-start(bf16[192,2048]{1,0:T(8,128)(2,1)} %param.7) | copy-start | bytes 2359300
  58.2 90.2 %all-gather.7.cloned.1.call-start = ((), (), s32[]{:S(2)}) async-start(), calls=%async_computation.4 | async-start | bytes 3932160 | tf_op jit(solution)/shard_map/all_gather | solution.py:40
  119.7 67.1 %all-gather.9.cloned.1.call-start = ((), (), s32[]{:S(2)}) async-start(), calls=%async_computation.6 | async-start | bytes 1966080 | tf_op jit(solution)/shard_map/all_gather | solution.py:21
  120.3 95.4 %all-gather.11.cloned.1.call-start = ((), (), s32[]{:S(2)}) async-start(), calls=%async_computation.7 | async-start | bytes 3932160 | tf_op jit(solution)/shard_map/all_gather | solution.py:39
  120.9 157.4 %reduce-scatter.5.cloned.1.call-start = ((), (), s32[]{:S(2)}) async-start(), calls=%async_computation.5 | async-start | bytes 3932160 | tf_op jit(solution)/shard_map/reduce_scatter | solution.py:43
  156.7 30.2 %copy-start.1 = (bf16[768,2048]{1,0:T(8,128)(2,1)S(1)}, bf16[768,2048]{1,0:T(8,128)(2,1)}, u32[]{:S(2)}) copy-start(bf16[768,2048]{1,0:T(8,128)(2,1)} %all-gather.7.cloned.1.call-done) | copy-start | bytes 9437188
  194.0 21.7 %copy-start.2 = (bf16[768,1024]{1,0:T(8,128)(2,1)S(1)}, bf16[768,1024]{1,0:T(8,128)(2,1)}, u32[]{:S(2)}) copy-start(bf16[768,1024]{1,0:T(8,128)(2,1)} %all-gather.5.cloned.1.call-done) | copy-start | bytes 4718596
Sparse Core Ops, SparseCore 0:
  9.5 39.7 all-gather.4
  58.3 57.7 reduce-scatter.2
  119.9 28.4 all-gather.6
  149.8 37.0 all-gather.8
  188.3 27.3 all-gather.10
  217.9 60.3 reduce-scatter.4
where the time goes:
time: 287 us
  waiting for transfers between devices  226 us (79%)
  matrix products  31.8 us (11%)
  between operations  14.1 us (5%)
  local copies, waits for them, and re-layouts  9.45 us (3%)
  other arithmetic  5.61 us (2%)
    reduce_scatter x1, waiting for transfers between devices, per_device(): lax.psum_scatter(lax.dot_general(piece, down_weight, last_dims, preferred...  57.8 us
    reduce_scatter x1, waiting for transfers between devices, per_device(): lax.psum_scatter(lax.dot_general(piece, up_weight, last_dims, preferred_e...  55 us
    all_gather x1, waiting for transfers between devices, per_device(): lax.all_gather(cotangent, 'col', axis=0, tiled=True)  41.4 us
    all_gather x1, waiting for transfers between devices, per_device(): lax.all_gather(inputs, 'col', axis=0, tiled=True)  30.2 us
    all_gather x1, waiting for transfers between devices, per_device(): lax.all_gather(pre_grad, 'row', axis=0, tiled=True)  27.4 us
    all_gather x1, waiting for transfers between devices, per_device(): lax.all_gather(activation, 'row', axis=0, tiled=True)  12.3 us
    unnamed x7, local copies, waits for them, and re-layouts  9.45 us
    dot_general x1, matrix products, per_device(): lax.dot_general(piece, down_weight, last_dims, preferred_element_type=jnp...  8.82 us
  transfers between devices with their start and end apart: 6, of which 6 were waited for; matrix products, arithmetic and copies ran while one was open for 11% of the time, Pallas kernels for 0%

commit v1 on v0

--- a/solution.py
+++ b/solution.py
@@ -3,6 +3,7 @@
 import jax.numpy as jnp
 from jax import lax
 from jax.sharding import PartitionSpec as P
+from jax.lax import axis_index, axis_size, ppermute
 
 
 def gelu_pair(values):
@@ -17,9 +18,39 @@
 
 
 def per_device(inputs, cotangent, preactivation, up_weight, down_weight):
+
+    def works_turn(tile_in):
+        lane_axis = "col"
+        carry_out, earlier, u1 = (axis_size(lane_axis), axis_index(lane_axis), tile_in.shape[0])
+        k_now = lax.dynamic_update_slice_in_dim(
+            jnp.zeros(
+                tuple((k * carry_out if w == 0 else k for w, k in enumerate(tile_in.shape))),
+                tile_in.dtype,
+            ),
+            tile_in,
+            earlier * u1,
+            axis=0,
+        )
+        t1 = formed = tile_in
+        for d in range(1, carry_out // 2 + 1):
+            t1 = ppermute(
+                t1, lane_axis, tuple(((w, (w + 1) % carry_out) for w in range(carry_out)))
+            )
+            k_now = lax.dynamic_update_slice_in_dim(
+                k_now, t1, (earlier - d) % carry_out * u1, axis=0
+            )
+            if 2 * d < carry_out:
+                formed = ppermute(
+                    formed, lane_axis, tuple(((w, (w - 1) % carry_out) for w in range(carry_out)))
+                )
+                k_now = lax.dynamic_update_slice_in_dim(
+                    k_now, formed, (earlier + d) % carry_out * u1, axis=0
+                )
+        return k_now
+
     inputs_all, cotangent_all = (
         lax.all_gather(inputs, "col", axis=0, tiled=True),
-        lax.all_gather(cotangent, "col", axis=0, tiled=True),
+        works_turn(cotangent),
     )
     total_tokens = inputs_all.shape[0]
     token_scale = 1.0 / math.sqrt(total_tokens)

time: 287 us -> 274 us (0.955)
  waiting for transfers between devices: 226 us -> 208 us
  starting transfers between devices: 0.24 us -> 5.58 us
    all_gather x1 -> x0, waiting for transfers between devices: 41.4 us -> none  [per_device(): lax.all_gather(cotangent, 'col', axis=0, tiled=True)]
    ppermute x0 -> x3, waiting for transfers between devices: none -> 25.8 us  [the longest x2 18.9 us: works_turn(): ppermute(t1, lane_axis, tuple(((w, (w + 1) % carry_out) for w in range(ca...]
    ppermute x0 -> x3, starting transfers between devices: none -> 5.2 us  [the longest x2 3.11 us: works_turn(): ppermute(t1, lane_axis, tuple(((w, (w + 1) % carry_out) for w in range(ca...]
    dot_general x1, matrix products: 8.82 us -> 5.43 us  [per_device(): lax.dot_general(piece, down_weight, last_dims, preferred_element_type=jnp...]
  transfers between devices with their start and end apart: 6 -> 8, of which waited for: 6 -> 8; matrix products, arithmetic and copies ran while one was open for 11% -> 13% of each run, Pallas kernels for 0% -> 0%
where the time goes in v1:
time: 274 us; the launch traced here: 273 us
  waiting for transfers between devices  208 us (76%)
  matrix products  30.8 us (11%)
  between operations  13.8 us (5%)
  local copies, waits for them, and re-layouts  9.46 us (3%)
  other arithmetic  5.61 us (2%)
  starting transfers between devices  5.58 us (2%)
    reduce_scatter x1, waiting for transfers between devices, per_device(): lax.psum_scatter(lax.dot_general(piece, down_weight, last_dims, preferred...  58.3 us
    reduce_scatter x1, waiting for transfers between devices, per_device(): lax.psum_scatter(lax.dot_general(piece, up_weight, last_dims, preferred_e...  55 us
    all_gather x1, waiting for transfers between devices, per_device(): lax.all_gather(inputs, 'col', axis=0, tiled=True)  30.3 us
    all_gather x1, waiting for transfers between devices, per_device(): lax.all_gather(pre_grad, 'row', axis=0, tiled=True)  27.1 us
    ppermute x2, waiting for transfers between devices, works_turn(): ppermute(t1, lane_axis, tuple(((w, (w + 1) % carry_out) for w in range(ca...  18.9 us
    all_gather x1, waiting for transfers between devices, per_device(): lax.all_gather(activation, 'row', axis=0, tiled=True)  10.2 us
    dot_general x1, matrix products, per_device(): lax.dot_general(inputs_all, pre_grad_all, first_dims, preferred_element_t...  9.53 us
    unnamed x7, local copies, waits for them, and re-layouts  9.14 us
  transfers between devices with their start and end apart: 8, of which 8 were waited for; matrix products, arithmetic and copies ran while one was open for 13% of the time, Pallas kernels for 0%

profile of v1, /device:TPU:0, one launch (start us, length us, event | category | flops | bytes accessed | tf_op | source)
XLA Modules:
  0.0 273.3 jit_solution(12929812969807383026)
XLA Ops:
  7.2 0.0 copy-start.1
  7.2 0.0 reduce-scatter.3.cloned.1.call-start
  7.2 3.1 %collective-permute-start = (bf16[192,1024]{1,0:T(8,128)(2,1)}, bf16[192,1024]{1,0:T(8,128)(2,1)S(1)}, u32[]{:S(2)}, u32[]{:S(2)}) collective-permute-start(bf16[192,1024]{1,0:T(8,128)(2,1)} %param.6), channel_id=1, source_target_pairs={{0,1},{1,2},{2,3},{3,0},{4,5},{5,6},{6,7},{7,4},{8,9},{9,10},{10,1... | collective-permute-start | bytes 1179656 | tf_op jit(solution)/shard_map/ppermute | solution.py:36
  10.3 2.1 collective-permute-start.1
  12.4 10.2 %collective-permute-done = bf16[192,1024]{1,0:T(8,128)(2,1)S(1)} collective-permute-done((bf16[192,1024]{1,0:T(8,128)(2,1)}, bf16[192,1024]{1,0:T(8,128)(2,1)S(1)}, u32[]{:S(2)}, u32[]{:S(2)}) %collective-permute-start) | collective-permute-done | bytes 393248 | tf_op jit(solution)/shard_map/ppermute | solution.py:36
  22.6 0.0 collective-permute-start.2
  22.6 0.2 broadcast_in_dim.3
  22.8 0.0 copy-done.1
  22.9 6.9 %collective-permute-done.1 = bf16[192,1024]{1,0:T(8,128)(2,1)S(1)} collective-permute-done((bf16[192,1024]{1,0:T(8,128)(2,1)}, bf16[192,1024]{1,0:T(8,128)(2,1)S(1)}, u32[]{:S(2)}, u32[]{:S(2)}) %collective-permute-start.1) | collective-permute-done | bytes 393248 | tf_op jit(solution)/shard_map/ppermute | solution.py:43
  29.8 8.8 %collective-permute-done.2 = bf16[192,1024]{1,0:T(8,128)(2,1)S(1)} collective-permute-done((bf16[192,1024]{1,0:T(8,128)(2,1)S(1)}, bf16[192,1024]{1,0:T(8,128)(2,1)S(1)}, u32[]{:S(2)}, u32[]{:S(2)}) %collective-permute-start.2) | collective-permute-done | bytes 393248 | tf_op jit(solution)/shard_map/ppermute | solution.py:36
  38.6 0.0 copy-done.2
  38.6 5.4 %fusion.11 = f32[768,2048]{1,0:T(8,128)} fusion(bf16[768,1024]{1,0:T(8,128)(2,1)S(1)} %constant_dynamic-update-slice_fusion, bf16[2048,1024]{1,0:T(8,128)(2,1)S(1)} %copy-done.2), kind=kOutput, calls=%fused_computation.24 | convolution fusion | flops 3221225472 | bytes 12058624 | tf_op jit(solution)/shard_map/dot_general | solution.py:61
  44.1 0.0 reduce-scatter.3.cloned.1.call-update
  44.1 0.0 all-gather.4.cloned.1.call-start
  44.1 58.3 %reduce-scatter.3.cloned.1.call-done = f32[192,2048]{1,0:T(8,128)} async-done(((f32[768,2048]{1,0:T(8,128)}), f32[192,2048]{1,0:T(8,128)}) %reduce-scatter.3.cloned.1.call-update) | async-done | bytes 1572880 | tf_op jit(solution)/shard_map/reduce_scatter | solution.py:60
  102.4 3.7 %fusion.7 = (bf16[192,2048]{1,0:T(8,128)(2,1)}, bf16[192,2048]{1,0:T(8,128)(2,1)}) fusion(bf16[192,2048]{1,0:T(8,128)(2,1)S(1)} %copy-done, f32[192,2048]{1,0:T(8,128)} %reduce-scatter.3.cloned.1.call-done), kind=kLoop, calls=%fused_computation.16 | loop fusion | flops 8650752 | bytes 3932160 | tf_op jit(solution)/shard_map/convert_element_type | solution.py:67
  106.1 0.0 all-gather.4.cloned.1.call-update
  106.1 0.0 all-gather.6.cloned.1.call-start
  106.2 0.7 all-gather.6.cloned.1.call-update
  106.9 0.0 all-gather.8.cloned.1.call-start
  106.9 0.5 all-gather.8.cloned.1.call-update
  107.4 0.2 reduce-scatter.5.cloned.1.call-start
  107.7 27.1 %all-gather.4.cloned.1.call-done = bf16[768,2048]{1,0:T(8,128)(2,1)} async-done(((bf16[192,2048]{1,0:T(8,128)(2,1)}), bf16[768,2048]{1,0:T(8,128)(2,1)}) %all-gather.4.cloned.1.call-update) | async-done | bytes 3145744 | tf_op jit(solution)/shard_map/all_gather | solution.py:71
  134.8 8.3 %fusion.12 = f32[768,1024]{1,0:T(8,128)} fusion(bf16[768,2048]{1,0:T(8,128)(2,1)} %all-gather.4.cloned.1.call-done, bf16[1024,2048]{1,0:T(8,128)(2,1)} %param.8), kind=kOutput, calls=%fused_computation.25 | convolution fusion | flops 3221225472 | bytes 10485760 | tf_op jit(solution)/shard_map/dot_general | solution.py:75
  143.1 0.0 reduce-scatter.5.cloned.1.call-update
  143.1 30.3 %all-gather.6.cloned.1.call-done = bf16[768,1024]{1,0:T(8,128)(2,1)} async-done(((bf16[192,1024]{1,0:T(8,128)(2,1)}), bf16[768,1024]{1,0:T(8,128)(2,1)}) %all-gather.6.cloned.1.call-update) | async-done | bytes 1572880 | tf_op jit(solution)/shard_map/all_gather | solution.py:52
  173.4 9.5 %multiply_bitcast_fusion = f32[1024,2048]{0,1:T(8,128)} fusion(bf16[768,2048]{1,0:T(8,128)(2,1)} %all-gather.4.cloned.1.call-done, bf16[768,1024]{1,0:T(8,128)(2,1)} %all-gather.6.cloned.1.call-done), kind=kOutput, calls=%fused_computation | convolution fusion | flops 3223322624 | bytes 13107200 | tf_op jit(solution)/shard_map/dot_general | solution.py:81
  183.0 9.1 %copy.8 = f32[1024,2048]{1,0:T(8,128)} copy(f32[1024,2048]{0,1:T(8,128)} %multiply_bitcast_fusion) | data formatting | bytes 16777216
  192.1 10.2 %all-gather.8.cloned.1.call-done = bf16[768,2048]{1,0:T(8,128)(2,1)} async-done(((bf16[192,2048]{1,0:T(8,128)(2,1)}), bf16[768,2048]{1,0:T(8,128)(2,1)}) %all-gather.8.cloned.1.call-update) | async-done | bytes 3145744 | tf_op jit(solution)/shard_map/all_gather | solution.py:70
  202.3 7.6 %convolution_multiply_fusion = f32[2048,1024]{1,0:T(8,128)} fusion(bf16[768,2048]{1,0:T(8,128)(2,1)} %all-gather.8.cloned.1.call-done, bf16[768,1024]{1,0:T(8,128)(2,1)S(1)} %constant_dynamic-update-slice_fusion), kind=kOutput, calls=%fused_computation.1 | convolution fusion | flops 3223322624 | bytes 13107200 | tf_op jit(solution)/shard_map/dot_general | solution.py:85
  209.9 55.0 %reduce-scatter.5.cloned.1.call-done = f32[192,1024]{1,0:T(8,128)} async-done(((f32[768,1024]{1,0:T(8,128)}), f32[192,1024]{1,0:T(8,128)}) %reduce-scatter.5.cloned.1.call-update) | async-done | bytes 786448 | tf_op jit(solution)/shard_map/reduce_scatter | solution.py:74
  264.8 1.9 convert_element_type.14
  (7 shorter events, 0.1 us)
Async XLA Ops:
  7.2 15.6 %copy-start.1 = (bf16[192,1024]{1,0:T(8,128)(2,1)S(1)}, bf16[192,1024]{1,0:T(8,128)(2,1)}, u32[]{:S(2)}) copy-start(bf16[192,1024]{1,0:T(8,128)(2,1)} %param.6) | copy-start | bytes 1179652
  7.2 95.3 %reduce-scatter.3.cloned.1.call-start = ((), (), s32[]{:S(2)}) async-start(), calls=%async_computation.2 | async-start | bytes 7864320 | tf_op jit(solution)/shard_map/reduce_scatter | solution.py:60
  7.2 15.3 %collective-permute-start = (bf16[192,1024]{1,0:T(8,128)(2,1)}, bf16[192,1024]{1,0:T(8,128)(2,1)S(1)}, u32[]{:S(2)}, u32[]{:S(2)}) collective-permute-start(bf16[192,1024]{1,0:T(8,128)(2,1)} %param.6), channel_id=1, source_target_pairs={{0,1},{1,2},{2,3},{3,0},{4,5},{5,6},{6,7},{7,4},{8,9},{9,10},{10,1... | collective-permute-start | bytes 1179656 | tf_op jit(solution)/shard_map/ppermute | solution.py:36
  10.3 19.5 %collective-permute-start.1 = (bf16[192,1024]{1,0:T(8,128)(2,1)}, bf16[192,1024]{1,0:T(8,128)(2,1)S(1)}, u32[]{:S(2)}, u32[]{:S(2)}) collective-permute-start(bf16[192,1024]{1,0:T(8,128)(2,1)} %param.6), channel_id=1, source_target_pairs={{0,3},{1,0},{2,1},{3,2},{4,7},{5,4},{6,5},{7,6},{8,11},{9,8},{10,9... | collective-permute-start | bytes 1179656 | tf_op jit(solution)/shard_map/ppermute | solution.py:43
  22.6 16.0 %collective-permute-start.2 = (bf16[192,1024]{1,0:T(8,128)(2,1)S(1)}, bf16[192,1024]{1,0:T(8,128)(2,1)S(1)}, u32[]{:S(2)}, u32[]{:S(2)}) collective-permute-start(bf16[192,1024]{1,0:T(8,128)(2,1)S(1)} %collective-permute-done), channel_id=1, source_target_pairs={{0,1},{1,2},{2,3},{3,0},{4,5},{5,6},{6,7},{7,4},{8,9},{9,10},{10,1... | collective-permute-start | bytes 1179656 | tf_op jit(solution)/shard_map/ppermute | solution.py:36
  22.6 16.0 %copy-start.2 = (bf16[2048,1024]{1,0:T(8,128)(2,1)S(1)}, bf16[2048,1024]{1,0:T(8,128)(2,1)}, u32[]{:S(2)}) copy-start(bf16[2048,1024]{1,0:T(8,128)(2,1)} %param.9) | copy-start | bytes 12582916
  44.1 58.4 %copy-start = (bf16[192,2048]{1,0:T(8,128)(2,1)S(1)}, bf16[192,2048]{1,0:T(8,128)(2,1)}, u32[]{:S(2)}) copy-start(bf16[192,2048]{1,0:T(8,128)(2,1)} %param.7) | copy-start | bytes 2359300
  44.1 90.7 %all-gather.4.cloned.1.call-start = ((), (), s32[]{:S(2)}) async-start(), calls=%async_computation.3 | async-start | bytes 3932160 | tf_op jit(solution)/shard_map/all_gather | solution.py:71
  106.1 67.3 %all-gather.6.cloned.1.call-start = ((), (), s32[]{:S(2)}) async-start(), calls=%async_computation.5 | async-start | bytes 1966080 | tf_op jit(solution)/shard_map/all_gather | solution.py:52
  106.9 95.4 %all-gather.8.cloned.1.call-start = ((), (), s32[]{:S(2)}) async-start(), calls=%async_computation.6 | async-start | bytes 3932160 | tf_op jit(solution)/shard_map/all_gather | solution.py:70
  107.4 157.4 %reduce-scatter.5.cloned.1.call-start = ((), (), s32[]{:S(2)}) async-start(), calls=%async_computation.4 | async-start | bytes 3932160 | tf_op jit(solution)/shard_map/reduce_scatter | solution.py:74
Sparse Core Ops, SparseCore 0:
  44.2 58.1 reduce-scatter.2
  106.3 28.5 all-gather.3
  136.4 37.0 all-gather.5
  174.9 27.3 all-gather.7
  204.4 60.3 reduce-scatter.4
